TPU v7x, 768 devices: a whole 4x8x12 slice. The times are simulated.
768 devices in a mesh: depth: 32 (over y, x), rows: 24 (over z, core).
Axes of the slice: x: 4, y: 8, z: 12, core: 2. Of those that a mesh axis runs over, the one named last changes fastest.
Arguments:
- volume: int32 [2, 256, 768, 1024], P(None, 'depth', 'rows'), may hold values from 0 to 255
- color_map: int32 [3, 256], replicated, may hold values from 0 to 255
- alpha_map: int32 [256], replicated, may hold values from 0 to 255
Outputs:
- image: float32 [4, 768, 1024], P(None, ('rows', 'depth'))
All inputs are finite; a program needn't handle non-finite values.
Results may differ from a plain program's by a relative error of at most 0.003.
Values may be sent and summed in bfloat16 or wider, within the bound.
A program may use at most 64 MiB of HBM per device.

v0:
```python
import jax
import jax.numpy as jnp
from jax import lax
from jax.sharding import PartitionSpec as P

LIGHT_DEPTH = 0.48
LIGHT_ROWS = 0.6
LIGHT_COLS = 0.64
OPACITY = 4.0


def with_halo(value, sides, width):
    for axis, dim in sides:
        size, length = (lax.axis_size(axis), value.shape[dim])
        up = [(i, (i + 1) % size) for i in range(size - 1)]
        down = [(j, i) for i, j in up]
        last = lax.slice_in_dim(value, length - width, length, axis=dim)
        first = lax.slice_in_dim(value, 0, width, axis=dim)
        before = lax.ppermute(last, axis, up)
        after = lax.ppermute(first, axis, down)
        value = jnp.concatenate([before, value, after], axis=dim)
    return value


def carried_in(value, axis, combine, identity):
    length, position = (lax.axis_size(axis), lax.axis_index(axis))
    everything = lax.all_gather(value.astype(jnp.bfloat16), axis)
    start = jnp.broadcast_to(jnp.asarray(identity, value.dtype), value.shape)

    def hop(k, before):
        reached = k < position
        new = combine(before, everything[k].astype(value.dtype))
        return jnp.where(reached, new, before)

    return lax.fori_loop(0, length, hop, start)


def spread_2(value, axis, root):
    mine = lax.axis_index(axis) == root
    return lax.psum(jnp.where(mine, value, jnp.zeros_like(value)), axis)


def composite(nearer, farther):
    remaining = 1.0 - nearer[3:4]
    return nearer + remaining * farther


def body(volume, color_map, alpha_map):
    depth_count = lax.axis_size("depth")
    slices = volume.shape[1]
    height = volume.shape[2]
    columns = volume.shape[3]
    voxel_count = height * columns
    primary = volume[0]
    secondary = volume[1]
    padded = with_halo(primary.astype(jnp.bfloat16), (("depth", 0), ("rows", 1)), 1)
    padded = jnp.pad(padded.astype(jnp.float32), ((0, 0), (0, 0), (1, 1)))
    grad_depth = 0.5 * (padded[2:, 1:-1, 1:-1] - padded[:-2, 1:-1, 1:-1])
    grad_rows = 0.5 * (padded[1:-1, 2:, 1:-1] - padded[1:-1, :-2, 1:-1])
    grad_cols = 0.5 * (padded[1:-1, 1:-1, 2:] - padded[1:-1, 1:-1, :-2])
    magnitude = jnp.sqrt(grad_depth * grad_depth + grad_rows * grad_rows + grad_cols * grad_cols)
    facing = LIGHT_DEPTH * grad_depth + LIGHT_ROWS * grad_rows + LIGHT_COLS * grad_cols
    shading_all = 0.3 + 0.7 * jnp.abs(facing) / jnp.maximum(magnitude, 1.0)
    levels = color_map.shape[1]
    high_count = levels // 32
    color_rows = color_map.astype(jnp.bfloat16).reshape(3 * high_count, 32)
    alpha_rows = alpha_map.astype(jnp.bfloat16).reshape(high_count, 32)
    low_levels = jnp.arange(32, dtype=jnp.int32)[:, None]
    high_levels = jnp.arange(high_count, dtype=jnp.int32)[:, None]
    opacity_scale = OPACITY / (255.0 * slices * depth_count)

    def lookup(lookup_table, level_slice, channels):
        flattened = level_slice.reshape(1, voxel_count)
        onehot = (flattened % 32 == low_levels).astype(jnp.bfloat16)
        spread = jnp.dot(lookup_table, onehot, preferred_element_type=jnp.float32).reshape(
            channels, high_count, voxel_count
        )
        selector = (flattened // 32 == high_levels).astype(jnp.float32)
        return jnp.sum(spread * selector[None], axis=1)

    def march_slice(slice_index, running):
        color_sum, alpha_sum = running
        primary_level = lax.dynamic_index_in_dim(primary, slice_index, 0, keepdims=False)
        secondary_level = lax.dynamic_index_in_dim(secondary, slice_index, 0, keepdims=False)
        emitted = lookup(color_rows, primary_level, 3) / 255.0
        opacity = lookup(alpha_rows, secondary_level, 1)[0] * opacity_scale
        shading = lax.dynamic_index_in_dim(shading_all, slice_index, 0, keepdims=False).reshape(
            voxel_count
        )
        weight = 1.0 - alpha_sum
        color_sum = color_sum + weight[None] * emitted * (opacity * shading)[None]
        alpha_sum = alpha_sum + weight * opacity
        return (color_sum, alpha_sum)

    starting = (jnp.zeros((3, voxel_count), jnp.float32), jnp.zeros((voxel_count,), jnp.float32))
    color_sum, alpha_sum = lax.fori_loop(0, slices, march_slice, starting)
    partial_image = jnp.concatenate([color_sum, alpha_sum[None]], axis=0).reshape(
        4, height, columns
    )
    row_share = height // depth_count
    prefix = carried_in(partial_image, "depth", composite, jnp.zeros_like(partial_image))
    finished_image = spread_2(composite(prefix, partial_image), "depth", depth_count - 1)
    return lax.dynamic_slice_in_dim(
        finished_image, lax.axis_index("depth") * row_share, row_share, 1
    )


def solution(mesh):
    in_specs = (P(None, "depth", "rows", None), P(), P())
    out_specs = P(None, ("rows", "depth"), None)
    return jax.shard_map(body, mesh=mesh, in_specs=in_specs, out_specs=out_specs, check_vma=False)
```

profile of v0, /device:TPU:6, one launch (start us, length us, event | category | flops | bytes accessed | tf_op | source)
XLA Modules:
  0.0 403.8 jit_solution(5419052687485249372)
XLA Ops:
  6.5 1.8 fusion.20
  8.4 3.4 collective-permute-start
  11.8 2.4 collective-permute-start.1
  14.5 5.5 %collective-permute-done.1 = bf16[1,32,1024]{2,1,0:T(8,128)(2,1)S(1)} collective-permute-done((bf16[1,32,1024]{2,1,0:T(8,128)(2,1)S(1)}, bf16[1,32,1024]{2,1,0:T(8,128)(2,1)S(1)}, u32[]{:S(2)}, u32[]{:S(2)}) %collective-permute-start.1) | collective-permute-done | bytes 65568 | tf_op jit(solution)/shard_map/ppermute | solution.py:20
  20.1 1.3 collective-permute-start.2
  21.4 1.3 collective-permute-start.3
  23.0 4.3 %collective-permute-done.3 = bf16[10,1,1024]{2,1,0:T(2,128)(2,1)} collective-permute-done((bf16[10,1,1024]{2,1,0:T(2,128)(2,1)S(1)}, bf16[10,1,1024]{2,1,0:T(2,128)(2,1)}, u32[]{:S(2)}, u32[]{:S(2)}) %collective-permute-start.3) | collective-permute-done | bytes 20512 | tf_op jit(solution)/shard_map/ppermute | solution.py:20
  28.4 2.5 divide_add_fusion
  30.8 36.5 %while.35 = (s32[]{:T(128)}, f32[3,32768]{1,0:T(4,128)S(1)}, f32[32768]{0:T(1024)S(1)}, s32[8,32,1024]{2,1,0:T(8,128)S(1)}, bf16[24,32]{1,0:T(8,128)(2,1)S(1)}, ...) while((s32[]{:T(128)}, f32[3,32768]{1,0:T(4,128)S(1)}, ...), condition=%wide.region_3.4_spmd.clone.clone, body=%wide.region_0.3_spmd.clone.clone.sunk | while | flops 73826304 | bytes 7735416 | solution.py:96
  33.3 1.7 fusion.34
  37.8 1.7 fusion.34
  42.4 1.7 fusion.34
  47.0 1.7 fusion.34
  51.5 1.7 fusion.34
  56.1 1.7 fusion.34
  60.7 1.7 fusion.34
  65.2 1.7 fusion.34
  68.7 116.1 %all-gather.2.cloned.1.call-done = bf16[32,4,32,1024]{3,2,1,0:T(8,128)(2,1)} async-done(((bf16[1,4,32,1024]{3,2,1,0:T(8,128)(2,1)}), bf16[32,4,32,1024]{3,2,1,0:T(8,128)(2,1)}) %all-gather.2.cloned.1.call-update) | async-done | bytes 8388624 | tf_op jit(solution)/shard_map/all_gather | solution.py:27
  184.9 42.2 %while.34 = (s32[]{:T(128)}, f32[4,32,1024]{2,1,0:T(8,128)S(1)}, s32[]{:T(128)}, bf16[32,4,32,1024]{3,2,1,0:T(8,128)(2,1)}, s32[]{:T(128)}, /*index=5*/s32[]{:T(128)}) while((s32[]{:T(128)}, f32[4,32,1024]{2,1,0:T(8,128)S(1)}, s32[]{:T(128)}, bf16[32,4,32,1024]{3,2,1,0:T(8,128)(2,1)}, s32[]{:T(128)}, /*index=5*/s32[]{:T(128)}) %tuple.93), condition=%wide.region_5.6_spmd.clone, body=%wide.region_4.5_spmd.clone.sunk | while | flops 819204 | bytes 2752606 | solution.py:35
  184.9 1.2 add_select_fusion.8
  186.3 1.2 add_select_fusion.8
  187.6 1.2 add_select_fusion.8
  188.9 1.2 add_select_fusion.8
  190.2 1.2 add_select_fusion.8
  191.5 1.2 add_select_fusion.8
  192.9 1.2 add_select_fusion.8
  194.2 1.2 add_select_fusion.8
  195.5 1.2 add_select_fusion.8
  196.8 1.2 add_select_fusion.8
  198.1 1.2 add_select_fusion.8
  199.5 1.2 add_select_fusion.8
  200.8 1.2 add_select_fusion.8
  202.1 1.2 add_select_fusion.8
  203.4 1.2 add_select_fusion.8
  204.7 1.2 add_select_fusion.8
  206.1 1.2 add_select_fusion.8
  207.4 1.2 add_select_fusion.8
  208.7 1.2 add_select_fusion.8
  210.0 1.2 add_select_fusion.8
  211.3 1.2 add_select_fusion.8
  212.7 1.2 add_select_fusion.8
  214.0 1.2 add_select_fusion.8
  215.3 1.2 add_select_fusion.8
  216.6 1.2 add_select_fusion.8
  219.3 1.2 add_select_fusion.8
  223.2 1.2 add_select_fusion.8
  228.0 167.4 %all-reduce.3.cloned.1.call-done = f32[4,32,1024]{2,1,0:T(8,128)} async-done(((f32[4,32,1024]{2,1,0:T(8,128)}), f32[4,32,1024]{2,1,0:T(8,128)}) %all-reduce.3.cloned.1.call-update) | async-done | bytes 524304 | tf_op jit(solution)/shard_map/psum | solution.py:40
  395.4 1.5 constant_dynamic-slice_fusion
  (186 shorter events, 34.0 us)
Async XLA Ops:
  6.5 16.2 %copy-start = (s32[3,256]{1,0:T(4,128)S(1)}, s32[3,256]{1,0:T(4,128)}, u32[]{:S(2)}) copy-start(s32[3,256]{1,0:T(4,128)} %param.8) | copy-start | bytes 9220
  6.5 16.3 %copy-start.1 = (s32[256]{0:T(256)S(1)}, s32[256]{0:T(256)}, u32[]{:S(2)}) copy-start(s32[256]{0:T(256)} %param.9) | copy-start | bytes 3076
  6.5 178.3 %all-gather.2.cloned.1.call-start = ((), (), s32[]{:S(2)}) async-start(), calls=%async_computation | async-start | bytes 8650752 | tf_op jit(solution)/shard_map/all_gather | solution.py:27
  8.4 6.2 %collective-permute-start = (bf16[1,32,1024]{2,1,0:T(8,128)(2,1)S(1)}, bf16[1,32,1024]{2,1,0:T(8,128)(2,1)S(1)}, u32[]{:S(2)}, u32[]{:S(2)}) collective-permute-start(bf16[1,32,1024]{2,1,0:T(8,128)(2,1)S(1)} %get-tuple-element.482), channel_id=1, source_target_pairs={{0,24},{24,48},{48,72},{72,96},{96,120},{120,144},{144,168},{168,1... | collective-permute-start | bytes 196616 | tf_op jit(solution)/shard_map/ppermute | solution.py:19
  11.8 8.3 %collective-permute-start.1 = (bf16[1,32,1024]{2,1,0:T(8,128)(2,1)S(1)}, bf16[1,32,1024]{2,1,0:T(8,128)(2,1)S(1)}, u32[]{:S(2)}, u32[]{:S(2)}) collective-permute-start(bf16[1,32,1024]{2,1,0:T(8,128)(2,1)S(1)} %get-tuple-element.483), channel_id=1, source_target_pairs={{24,0},{48,24},{72,48},{96,72},{120,96},{144,120},{168,144},{192,1... | collective-permute-start | bytes 196616 | tf_op jit(solution)/shard_map/ppermute | solution.py:20
  20.1 2.8 collective-permute-start.2
  21.4 5.9 %collective-permute-start.3 = (bf16[10,1,1024]{2,1,0:T(2,128)(2,1)S(1)}, bf16[10,1,1024]{2,1,0:T(2,128)(2,1)}, u32[]{:S(2)}, u32[]{:S(2)}) collective-permute-start(bf16[10,1,1024]{2,1,0:T(2,128)(2,1)S(1)} %get-tuple-element.481), channel_id=1, source_target_pairs={{1,0},{2,1},{3,2},{4,3},{5,4},{6,5},{7,6},{8,7},{9,8},{10,9},{11,1... | collective-permute-start | bytes 61448 | tf_op jit(solution)/shard_map/ppermute | solution.py:20
  68.4 327.0 %all-reduce.3.cloned.1.call-start = ((), (), s32[]{:S(2)}) async-start(), calls=%async_computation.1 | async-start | bytes 1048576 | tf_op jit(solution)/shard_map/psum | solution.py:40
Sparse Core Ops, SparseCore 0:
  68.5 116.3 all-gather.1
  228.1 167.2 all-reduce.2
where the time goes:
time: 406 us; the launch traced here: 404 us
  waiting for transfers between devices  294 us (72%)
  other arithmetic  55 us (14%)
  matrix products  20.8 us (5%)
  between operations  13.6 us (3%)
  local copies, waits for them, and re-layouts  10.3 us (3%)
  starting transfers between devices  8.47 us (2%)
    psum x1, waiting for transfers between devices, spread_2(): return lax.psum(jnp.where(mine, value, jnp.zeros_like(value)), axis)  167 us
    all_gather x1, waiting for transfers between devices, carried_in(): everything = lax.all_gather(value.astype(jnp.bfloat16), axis)  116 us
    select_n x32, other arithmetic, hop(): return jnp.where(reached, new, before)  39.4 us
    dot_general x16, matrix products, lookup(): jnp.dot(lookup_table, onehot, preferred_element_type=jnp.float32)  20.8 us
    ppermute x2, waiting for transfers between devices, with_halo(): after = lax.ppermute(first, axis, down)  9.84 us
    while x40, local copies, waits for them, and re-layouts  8.18 us
  transfers between devices with their start and end apart: 6, of which 5 were waited for; matrix products, arithmetic and copies ran while one was open for 0% of the time, Pallas kernels for 0%

commit v1 on v0

v1 whole, which is shorter than its diff:
```python
import functools

import jax
import jax.numpy as jnp
from jax import lax
from jax.experimental import pallas as pl
from jax.experimental.pallas import tpu as pltpu
from jax.sharding import PartitionSpec as P

LIGHT_DEPTH = 0.336
LIGHT_ROWS = 0.42
LIGHT_COLS = 0.448
OPACITY = 4.0
LANES = 128
SUBS = 8
MESH = pl.DeviceIdType.MESH
F32 = jnp.float32


def take(table, index):
    return jnp.take_along_axis(table, index, axis=1, mode="promise_in_bounds")


def kernel(
    slices, height, depth_count, row_count,
    volume, color_ref, alpha_ref, out_ref,
    first, second, row_halo, depth_halo, part, sent, got,
    load_sem, halo_send, halo_recv, send_sem, recv_sem,
):
    S, H, D, R = slices, height, depth_count, row_count
    d, r = lax.axis_index("depth"), lax.axis_index("rows")

    loads = []
    for p, buffer in enumerate((first, second)):
        for block in range(SUBS):
            source = volume.at[p, :, :, pl.ds(block * LANES, LANES)]
            target = buffer.at[:, pl.ds(1, H), block, :] if p == 0 else buffer.at[:, :, block, :]
            load = pltpu.make_async_copy(source, target, load_sem.at[p, block])
            load.start()
            loads.append(load)

    barrier = pltpu.get_barrier_semaphore()

    def greet(k, _):
        pl.semaphore_signal(
            barrier, inc=1, device_id=(lax.rem(d + k, D), r), device_id_type=MESH
        )
        return 0

    lax.fori_loop(1, D, greet, 0)

    @pl.when(r > 0)
    def _():
        pl.semaphore_signal(barrier, inc=1, device_id=(d, r - 1), device_id_type=MESH)

    @pl.when(r < R - 1)
    def _():
        pl.semaphore_signal(barrier, inc=1, device_id=(d, r + 1), device_id_type=MESH)

    lane = lax.broadcasted_iota(jnp.int32, (SUBS, LANES), 1)
    sub = lax.broadcasted_iota(jnp.int32, (SUBS, LANES), 0)
    last_lane, first_lane = lane == LANES - 1, lane == 0
    not_last, not_first = (sub < SUBS - 1).astype(F32), (sub > 0).astype(F32)

    def spread(row):
        return jnp.broadcast_to(row, (SUBS, LANES))

    colors = color_ref[0:1] + color_ref[1:2] * 256 + color_ref[2:3] * 65536
    color_low, color_high = spread(colors[:, :LANES]), spread(colors[:, LANES:])
    alphas = spread(alpha_ref[0:1] + alpha_ref[1:2] * 256)

    zero = jnp.zeros((SUBS, LANES), jnp.int32)

    @pl.when(d == 0)
    def _():
        for i in range(H):
            depth_halo[0, i] = zero

    @pl.when(d == D - 1)
    def _():
        for i in range(H):
            depth_halo[1, i] = zero

    @pl.when(r == 0)
    def _():
        for s in range(S):
            row_halo[0, s] = zero

    @pl.when(r == R - 1)
    def _():
        for s in range(S):
            row_halo[1, s] = zero

    for load in loads[:SUBS]:
        load.wait()
    n_greet = D - 1 + (r > 0).astype(jnp.int32) + (r < R - 1).astype(jnp.int32)
    pl.semaphore_wait(barrier, n_greet)

    def halo(which, source, target, device):
        return pltpu.make_async_remote_copy(
            src_ref=source, dst_ref=target, send_sem=halo_send.at[which],
            recv_sem=halo_recv.at[which], device_id=device, device_id_type=MESH,
        )

    own = pl.ds(1, H)
    ahead = halo(0, first.at[S - 1, own], depth_halo.at[0], (d + 1, r))
    behind = halo(1, first.at[0, own], depth_halo.at[1], (d - 1, r))
    below = halo(2, first.at[:, H], row_halo.at[0], (d, r + 1))
    above = halo(3, first.at[:, 1], row_halo.at[1], (d, r - 1))
    halos = (
        (ahead, d < D - 1, d > 0), (behind, d > 0, d < D - 1),
        (below, r < R - 1, r > 0), (above, r > 0, r < R - 1),
    )
    for copy, sends, _ in halos:
        @pl.when(sends)
        def _(copy=copy):
            copy.start()

    for load in loads[SUBS:]:
        load.wait()

    def inner(row):
        clear = jnp.ones((SUBS, LANES), F32)
        total = [jnp.zeros((SUBS, LANES), F32)] * 3
        value = [first[s, row + 1] for s in range(S)]
        for s in range(S):
            level = second[s, row]
            code = take(alphas, level & 127)
            opacity = ((code >> ((level >> 4) & 8)) & 255).astype(F32) * (OPACITY / (255.0 * S * D))
            index = value[s] & 127
            code = jnp.where(value[s] >= 128, take(color_high, index), take(color_low, index))
            emitted = [(code & 255).astype(F32), ((code >> 8) & 255).astype(F32), (code >> 16).astype(F32)]
            here = value[s].astype(F32)
            right = pltpu.roll(here, LANES - 1, 1)
            left = pltpu.roll(here, 1, 1)
            right = jnp.where(last_lane, pltpu.roll(right, SUBS - 1, 0) * not_last, right)
            left = jnp.where(first_lane, pltpu.roll(left, 1, 0) * not_first, left)
            grad_cols = right - left
            grad_rows = (first[s, row + 2] - first[s, row]).astype(F32)
            facing = LIGHT_ROWS * grad_rows + LIGHT_COLS * grad_cols
            square = grad_rows * grad_rows + grad_cols * grad_cols
            weight = clear * opacity
            clear = clear - weight
            weight = weight * (1.0 / 255.0)
            if 0 < s < S - 1:
                grad_depth = (value[s + 1] - value[s - 1]).astype(F32)
                facing = facing + LIGHT_DEPTH * grad_depth
                square = square + grad_depth * grad_depth
                lit = weight * (0.3 + jnp.abs(facing) * lax.rsqrt(jnp.maximum(square, 4.0)))
                total = [t + e * lit for t, e in zip(total, emitted)]
            else:
                for i, x in enumerate([weight, facing, square] + emitted):
                    part[row, (4 if s == 0 else 10) + i] = x
        for i, x in enumerate(total + [1.0 - clear]):
            part[row, i] = x

    def inner_pair(i, _):
        inner(2 * i + 1)
        inner(2 * i + 2)
        return 0

    lax.fori_loop(0, (H - 2) // 2, inner_pair, 0)

    for copy, _, receives in halos[2:]:
        @pl.when(receives)
        def _(copy=copy):
            copy.wait_recv()
    for s in range(S):
        first[s, 0] = row_halo[0, s]
        first[s, H + 1] = row_halo[1, s]

    def inner_edge(i, _):
        inner(i * (H - 1))
        return 0

    lax.fori_loop(0, 2, inner_edge, 0)

    for copy, _, receives in halos[:2]:
        @pl.when(receives)
        def _(copy=copy):
            copy.wait_recv()

    def outer(row, buffer, slot):
        total = [part[row, i] for i in range(3)]
        for at, grad in (
            (4, first[1, row + 1] - depth_halo[0, row]),
            (10, depth_halo[1, row] - first[S - 2, row + 1]),
        ):
            grad = grad.astype(F32)
            facing = part[row, at + 1] + LIGHT_DEPTH * grad
            square = part[row, at + 2] + grad * grad
            lit = part[row, at] * (0.3 + jnp.abs(facing) * lax.rsqrt(jnp.maximum(square, 4.0)))
            total = [t + part[row, at + 3 + i] * lit for i, t in enumerate(total)]
        total.append(part[row, 3])
        for i in range(2):
            pair = jnp.concatenate(total[2 * i : 2 * i + 2], axis=0)
            buffer[slot, pl.ds(16 * i, 16)] = pair.astype(jnp.bfloat16)

    def shipment(row):
        return pltpu.make_async_remote_copy(
            src_ref=sent.at[row], dst_ref=got.at[d], send_sem=send_sem.at[row],
            recv_sem=recv_sem.at[d], device_id=(row, r), device_id_type=MESH,
        )

    def ship(k, _):
        row = lax.rem(d + k, D)
        outer(row, sent, row)
        shipment(row).start()
        return 0

    lax.fori_loop(1, D, ship, 0)
    outer(d, got, d)

    def arrive(k, _):
        peer = lax.rem(d + k, D)
        pltpu.make_async_remote_copy(
            src_ref=sent.at[peer], dst_ref=got.at[peer], send_sem=send_sem.at[peer],
            recv_sem=recv_sem.at[peer], device_id=(peer, r), device_id_type=MESH,
        ).wait_recv()
        return 0

    lax.fori_loop(1, D, arrive, 0)

    clear = jnp.ones((SUBS, LANES), F32)
    total = [jnp.zeros((SUBS, LANES), F32)] * 3
    for k in range(D):
        slab = got[k].astype(F32)
        total = [t + clear * slab[SUBS * i : SUBS * (i + 1)] for i, t in enumerate(total)]
        clear = clear - clear * slab[3 * SUBS :]
    for i, x in enumerate(total + [1.0 - clear]):
        out_ref[i] = x

    def drain(k, _):
        shipment(lax.rem(d + k, D)).wait_send()
        return 0

    lax.fori_loop(1, D, drain, 0)
    for copy, sends, _ in halos:
        @pl.when(sends)
        def _(copy=copy):
            copy.wait_send()


def body(volume, color_map, alpha_map):
    D, R = lax.axis_size("depth"), lax.axis_size("rows")
    S, H = volume.shape[1], volume.shape[2]
    vmem = pl.BlockSpec(memory_space=pltpu.VMEM)
    image = pl.pallas_call(
        functools.partial(kernel, S, H, D, R),
        out_shape=jax.ShapeDtypeStruct((4, SUBS, LANES), F32),
        in_specs=[pl.BlockSpec(memory_space=pl.ANY), vmem, vmem],
        out_specs=vmem,
        scratch_shapes=[
            pltpu.VMEM((S, H + 2, SUBS, LANES), jnp.int32),
            pltpu.VMEM((S, H, SUBS, LANES), jnp.int32),
            pltpu.VMEM((2, S, SUBS, LANES), jnp.int32),
            pltpu.VMEM((2, H, SUBS, LANES), jnp.int32),
            pltpu.VMEM((H, 16, SUBS, LANES), F32),
            pltpu.VMEM((D, 4 * SUBS, LANES), jnp.bfloat16),
            pltpu.VMEM((D, 4 * SUBS, LANES), jnp.bfloat16),
            pltpu.SemaphoreType.DMA((2, SUBS)),
            pltpu.SemaphoreType.DMA((4,)),
            pltpu.SemaphoreType.DMA((4,)),
            pltpu.SemaphoreType.DMA((D,)),
            pltpu.SemaphoreType.DMA((D,)),
        ],
        compiler_params=pltpu.CompilerParams(collective_id=0, has_side_effects=True),
        name="render",
    )(volume, color_map, alpha_map.reshape(2, LANES))
    return image.reshape(4, 1, SUBS * LANES)


def solution(mesh):
    in_specs = (P(None, "depth", "rows", None), P(), P())
    out_specs = P(None, ("rows", "depth"), None)
    return jax.shard_map(body, mesh=mesh, in_specs=in_specs, out_specs=out_specs, check_vma=False)
```

time: 406 us -> 30.5 us (0.08)
  waiting for transfers between devices: 294 us -> 0 us
  other arithmetic: 55 us -> 0 us
  Pallas kernels: 0 us -> 28.9 us
  matrix products: 20.8 us -> 0 us
  between operations: 13.6 us -> 0.01 us
  local copies, waits for them, and re-layouts: 10.3 us -> 1.32 us
  starting transfers between devices: 8.47 us -> 0 us
    psum x1 -> x0, waiting for transfers between devices: 167 us -> none  [spread_2(): return lax.psum(jnp.where(mine, value, jnp.zeros_like(value)), axis)]
    all_gather x1 -> x0, waiting for transfers between devices: 116 us -> none  [carried_in(): everything = lax.all_gather(value.astype(jnp.bfloat16), axis)]
    select_n x49 -> x0, other arithmetic: 42.1 us -> none  [the longest x32 39.4 us: hop(): return jnp.where(reached, new, before)]
    pallas_call x0 -> x1, Pallas kernels: none -> 28.9 us  [body(): pl.pallas_call(functools.partial(kernel, S, H, D, R), out_shape=jax.Shape...]
    dot_general x16 -> x0, matrix products: 20.8 us -> none  [lookup(): jnp.dot(lookup_table, onehot, preferred_element_type=jnp.float32)]
    ppermute x4 -> x0, waiting for transfers between devices: 10.1 us -> none  [the longest x2 9.84 us: with_halo(): after = lax.ppermute(first, axis, down)]
    ppermute x4 -> x0, starting transfers between devices: 8.43 us -> none  [the longest x2 4.69 us: with_halo(): before = lax.ppermute(last, axis, up)]
    while x40 -> x0, local copies, waits for them, and re-layouts: 8.18 us -> none
  transfers between devices with their start and end apart: 6 -> 0, of which waited for: 5 -> 0; matrix products, arithmetic and copies ran while one was open for 0% -> 0% of each run, Pallas kernels for 0% -> 0%
where the time goes in v1:
time: 30.5 us; the launch traced here: 30.3 us
  Pallas kernels  28.9 us (95%)
  local copies, waits for them, and re-layouts  1.32 us (4%)
    pallas_call x1, Pallas kernels, body(): pl.pallas_call(functools.partial(kernel, S, H, D, R), out_shape=jax.Shape...  28.9 us
    unnamed x1, local copies, waits for them, and re-layouts  1.32 us

profile of v1, /device:TPU:6, one launch (start us, length us, event | category | flops | bytes accessed | tf_op | source)
XLA Modules:
  0.0 30.3 jit_solution(9313597484949171710)
XLA Ops:
  0.0 28.9 %render.1 = f32[4,8,128]{2,1,0:T(8,128)} custom-call(s32[2,8,32,1024]{3,2,1,0:T(8,128)} %volume.1, s32[3,256]{1,0:T(4,128)} %color_ref.1, s32[2,128]{1,0:T(2,128)} %bitcast.3), custom_call_target="tpu_custom_call" | custom-call | tf_op jit(solution)/shard_map/render/pallas_call | solution.py:248
  28.9 1.3 %copy.6 = f32[4,1,1024]{2,1,0:T(1,128)} copy(f32[4,1,1024]{2,1,0:T(1,128)} %bitcast.2) | data formatting | bytes 32768

commit v2 on v1

--- a/solution.py
+++ b/solution.py
@@ -15,6 +15,8 @@
 SUBS = 8
 MESH = pl.DeviceIdType.MESH
 F32 = jnp.float32
+X = 4
+UNROLL = 5
 
 
 def take(table, index):
@@ -24,11 +26,41 @@
 def kernel(
     slices, height, depth_count, row_count,
     volume, color_ref, alpha_ref, out_ref,
-    first, second, row_halo, depth_halo, part, sent, got,
-    load_sem, halo_send, halo_recv, send_sem, recv_sem,
+    first, second, row_halo, depth_edge, depth_halo, part, sent, got,
+    load_sem, halo_send, halo_recv, send_sem, recv_sem, near_sem, far_sem,
 ):
     S, H, D, R = slices, height, depth_count, row_count
     d, r = lax.axis_index("depth"), lax.axis_index("rows")
+
+    Y = D // X
+    y, x = lax.div(d, X), lax.rem(d, X)
+    HALF = H // 2
+
+    def along(step):
+        return lax.rem(y + step + Y, Y) * X + x
+
+    barrier = pltpu.get_barrier_semaphore()
+
+    def greet(device):
+        pl.semaphore_signal(barrier, inc=1, device_id=device, device_id_type=MESH)
+
+    def greet_if(condition, device):
+        @pl.when(condition)
+        def _():
+            greet(device)
+
+    crosses_up, crosses_down = (x == X - 1) & (d < D - 1), (x == 0) & (d > 0)
+    greet_if(crosses_up, (d + 1, r))
+    greet_if(crosses_down, (d - 1, r))
+    for k in range(1, X):
+        greet((y * X + lax.rem(x + k, X), r))
+    for step in (1, -1, 2, -2):
+        greet((along(step), r))
+    greet_if(r > 0, (d, r - 1))
+    greet_if(r < R - 1, (d, r + 1))
+    n_greet = X + 3
+    for condition in (crosses_up, crosses_down, r > 0, r < R - 1):
+        n_greet = n_greet + condition.astype(jnp.int32)
 
     loads = []
     for p, buffer in enumerate((first, second)):
@@ -39,24 +71,6 @@
             load.start()
             loads.append(load)
 
-    barrier = pltpu.get_barrier_semaphore()
-
-    def greet(k, _):
-        pl.semaphore_signal(
-            barrier, inc=1, device_id=(lax.rem(d + k, D), r), device_id_type=MESH
-        )
-        return 0
-
-    lax.fori_loop(1, D, greet, 0)
-
-    @pl.when(r > 0)
-    def _():
-        pl.semaphore_signal(barrier, inc=1, device_id=(d, r - 1), device_id_type=MESH)
-
-    @pl.when(r < R - 1)
-    def _():
-        pl.semaphore_signal(barrier, inc=1, device_id=(d, r + 1), device_id_type=MESH)
-
     lane = lax.broadcasted_iota(jnp.int32, (SUBS, LANES), 1)
     sub = lax.broadcasted_iota(jnp.int32, (SUBS, LANES), 0)
     last_lane, first_lane = lane == LANES - 1, lane == 0
@@ -73,12 +87,12 @@
 
     @pl.when(d == 0)
     def _():
-        for i in range(H):
+        for i in range(HALF):
             depth_halo[0, i] = zero
 
     @pl.when(d == D - 1)
     def _():
-        for i in range(H):
+        for i in range(HALF):
             depth_halo[1, i] = zero
 
     @pl.when(r == 0)
@@ -93,7 +107,9 @@
 
     for load in loads[:SUBS]:
         load.wait()
-    n_greet = D - 1 + (r > 0).astype(jnp.int32) + (r < R - 1).astype(jnp.int32)
+    for i in range(HALF):
+        depth_edge[0, i] = first[S - 1, i + 1] + first[S - 1, i + 1 + HALF] * 65536
+        depth_edge[1, i] = first[0, i + 1] + first[0, i + 1 + HALF] * 65536
     pl.semaphore_wait(barrier, n_greet)
 
     def halo(which, source, target, device):
@@ -102,9 +118,8 @@
             recv_sem=halo_recv.at[which], device_id=device, device_id_type=MESH,
         )
 
-    own = pl.ds(1, H)
-    ahead = halo(0, first.at[S - 1, own], depth_halo.at[0], (d + 1, r))
-    behind = halo(1, first.at[0, own], depth_halo.at[1], (d - 1, r))
+    ahead = halo(0, depth_edge.at[0], depth_halo.at[0], (d + 1, r))
+    behind = halo(1, depth_edge.at[1], depth_halo.at[1], (d - 1, r))
     below = halo(2, first.at[:, H], row_halo.at[0], (d, r + 1))
     above = halo(3, first.at[:, 1], row_halo.at[1], (d, r - 1))
     halos = (
@@ -115,6 +130,25 @@
         @pl.when(sends)
         def _(copy=copy):
             copy.start()
+
+    for slot, side in ((1, 1), (0, -1)):
+        for hops in (1, 2):
+            pl.semaphore_signal(
+                near_sem.at[slot, hops - 1], inc=1,
+                device_id=(along(side * hops), r), device_id_type=MESH,
+            )
+    side = jnp.where(y <= Y // 2, 1, -1)
+    middle = (y == 0) | ((y >= Y // 2 - 1) & (y <= Y // 2 + 1))
+
+    def slot_of(side):
+        return lax.div(1 - side, 2)
+
+    def hear_near(side):
+        pl.semaphore_wait(near_sem.at[slot_of(side), 0], 1)
+        pl.semaphore_wait(near_sem.at[slot_of(side), 1], 1)
+        pl.semaphore_signal(
+            far_sem.at[slot_of(side)], inc=1, device_id=(along(-2 * side), r), device_id_type=MESH
+        )
 
     for load in loads[SUBS:]:
         load.wait()
@@ -154,12 +188,20 @@
         for i, x in enumerate(total + [1.0 - clear]):
             part[row, i] = x
 
-    def inner_pair(i, _):
-        inner(2 * i + 1)
-        inner(2 * i + 2)
+    def inner_group(i, _):
+        for k in range(UNROLL):
+            inner(UNROLL * i + 1 + k)
         return 0
 
-    lax.fori_loop(0, (H - 2) // 2, inner_pair, 0)
+    groups = (H - 2) // UNROLL
+    lax.fori_loop(0, groups // 2, inner_group, 0)
+    hear_near(side)
+
+    @pl.when(middle)
+    def _():
+        hear_near(-side)
+
+    lax.fori_loop(groups // 2, groups, inner_group, 0)
 
     for copy, _, receives in halos[2:]:
         @pl.when(receives)
@@ -169,11 +211,8 @@
         first[s, 0] = row_halo[0, s]
         first[s, H + 1] = row_halo[1, s]
 
-    def inner_edge(i, _):
-        inner(i * (H - 1))
-        return 0
-
-    lax.fori_loop(0, 2, inner_edge, 0)
+    for row in (0, H - 1):
+        inner(row)
 
     for copy, _, receives in halos[:2]:
         @pl.when(receives)
@@ -182,9 +221,11 @@
 
     def outer(row, buffer, slot):
         total = [part[row, i] for i in range(3)]
+        word, shift = lax.rem(row, HALF), lax.div(row, HALF) * 16
+        front, back = ((depth_halo[i, word] >> shift) & 255 for i in range(2))
         for at, grad in (
-            (4, first[1, row + 1] - depth_halo[0, row]),
-            (10, depth_halo[1, row] - first[S - 2, row + 1]),
+            (4, first[1, row + 1] - front),
+            (10, back - first[S - 2, row + 1]),
         ):
             grad = grad.astype(F32)
             facing = part[row, at + 1] + LIGHT_DEPTH * grad
@@ -202,14 +243,37 @@
             recv_sem=recv_sem.at[d], device_id=(row, r), device_id_type=MESH,
         )
 
-    def ship(k, _):
-        row = lax.rem(d + k, D)
+    outer(d, got, d)
+    for k in range(1, X):
+        row = y * X + lax.rem(x + k, X)
         outer(row, sent, row)
         shipment(row).start()
+
+    def ship(k, _):
+        late = jnp.where(k < 4, k + 2, jnp.where(k < 6, k - 4, k))
+        step = jnp.where(y == Y // 2, late, k)
+
+        @pl.when(step == 0)
+        def _():
+            pl.semaphore_wait(far_sem.at[slot_of(side)], 1)
+
+        @pl.when((step == 4) & jnp.logical_not(middle))
+        def _():
+            hear_near(-side)
+
+        @pl.when(step == 6)
+        def _():
+            pl.semaphore_wait(far_sem.at[slot_of(-side)], 1)
+
+        away = jnp.where(step < 2, step + 3, jnp.where(step < 4, step - 1, 3 - step))
+        base = lax.rem(y + away * side + Y, Y) * X
+        for i in range(X):
+            outer(base + i, sent, base + i)
+        for i in range(X):
+            shipment(base + i).start()
         return 0
 
-    lax.fori_loop(1, D, ship, 0)
-    outer(d, got, d)
+    lax.fori_loop(0, Y - 1, ship, 0)
 
     def arrive(k, _):
         peer = lax.rem(d + k, D)
@@ -247,14 +311,15 @@
     vmem = pl.BlockSpec(memory_space=pltpu.VMEM)
     image = pl.pallas_call(
         functools.partial(kernel, S, H, D, R),
-        out_shape=jax.ShapeDtypeStruct((4, SUBS, LANES), F32),
+        out_shape=pltpu.VMEM((4, SUBS, LANES), F32),
         in_specs=[pl.BlockSpec(memory_space=pl.ANY), vmem, vmem],
         out_specs=vmem,
         scratch_shapes=[
             pltpu.VMEM((S, H + 2, SUBS, LANES), jnp.int32),
             pltpu.VMEM((S, H, SUBS, LANES), jnp.int32),
             pltpu.VMEM((2, S, SUBS, LANES), jnp.int32),
-            pltpu.VMEM((2, H, SUBS, LANES), jnp.int32),
+            pltpu.VMEM((2, H // 2, SUBS, LANES), jnp.int32),
+            pltpu.VMEM((2, H // 2, SUBS, LANES), jnp.int32),
             pltpu.VMEM((H, 16, SUBS, LANES), F32),
             pltpu.VMEM((D, 4 * SUBS, LANES), jnp.bfloat16),
             pltpu.VMEM((D, 4 * SUBS, LANES), jnp.bfloat16),
@@ -263,6 +328,8 @@
             pltpu.SemaphoreType.DMA((4,)),
             pltpu.SemaphoreType.DMA((D,)),
             pltpu.SemaphoreType.DMA((D,)),
+            pltpu.SemaphoreType.REGULAR((2, 2)),
+            pltpu.SemaphoreType.REGULAR((2,)),
         ],
         compiler_params=pltpu.CompilerParams(collective_id=0, has_side_effects=True),
         name="render",

time: 30.5 us -> 26.2 us (0.86)
  Pallas kernels: 28.9 us -> 25.3 us
  local copies, waits for them, and re-layouts: 1.32 us -> 0.61 us
    pallas_call x1, Pallas kernels: 28.9 us -> 25.3 us  [body(): pl.pallas_call(functools.partial(kernel, S, H, D, R), out_shape=pltpu.VME...]
    unnamed x1, local copies, waits for them, and re-layouts: 1.32 us -> 0.61 us
where the time goes in v2:
time: 26.2 us; the launch traced here: 26 us
  Pallas kernels  25.3 us (97%)
  local copies, waits for them, and re-layouts  0.61 us (2%)
    pallas_call x1, Pallas kernels, body(): pl.pallas_call(functools.partial(kernel, S, H, D, R), out_shape=pltpu.VME...  25.3 us
    unnamed x1, local copies, waits for them, and re-layouts  0.61 us

profile of v2, /device:TPU:6, one launch (start us, length us, event | category | flops | bytes accessed | tf_op | source)
XLA Modules:
  0.0 26.0 jit_solution(13518888976488602350)
XLA Ops:
  0.0 25.3 %render.1 = f32[4,8,128]{2,1,0:T(8,128)S(1)} custom-call(s32[2,8,32,1024]{3,2,1,0:T(8,128)} %volume.1, s32[3,256]{1,0:T(4,128)} %color_ref.1, s32[2,128]{1,0:T(2,128)} %bitcast.3), custom_call_target="tpu_custom_call" | custom-call | tf_op jit(solution)/shard_map/render/pallas_call | solution.py:312
  25.4 0.6 %copy.6 = f32[4,1,1024]{2,1,0:T(1,128)} copy(f32[4,1,1024]{2,1,0:T(1,128)S(1)} %bitcast.2) | data formatting | bytes 32768

commit v3 on v2

--- a/solution.py
+++ b/solution.py
@@ -25,9 +25,9 @@
 
 def kernel(
     slices, height, depth_count, row_count,
-    volume, color_ref, alpha_ref, out_ref,
-    first, second, row_halo, depth_edge, depth_halo, part, sent, got,
-    load_sem, halo_send, halo_recv, send_sem, recv_sem, near_sem, far_sem,
+    volume, color_map, alpha_map, out_ref,
+    color_ref, alpha_ref, first, second, row_halo, depth_edge, depth_halo, part, sent, got, joined, met,
+    table_sem, load_sem, halo_send, halo_recv, sent_sem, got_sem, joined_sem, met_sem, news_sem, here_sem,
 ):
     S, H, D, R = slices, height, depth_count, row_count
     d, r = lax.axis_index("depth"), lax.axis_index("rows")
@@ -49,19 +49,33 @@
         def _():
             greet(device)
 
+    root = d == 0
     crosses_up, crosses_down = (x == X - 1) & (d < D - 1), (x == 0) & (d > 0)
     greet_if(crosses_up, (d + 1, r))
     greet_if(crosses_down, (d - 1, r))
-    for k in range(1, X):
-        greet((y * X + lax.rem(x + k, X), r))
-    for step in (1, -1, 2, -2):
-        greet((along(step), r))
+    greet_if(root, (d + 1, r))
+
+    @pl.when(jnp.logical_not(root))
+    def _():
+        for k in range(1, X):
+            greet((y * X + lax.rem(x + k, X), r))
+        for step in (1, -1, 2, -2):
+            greet((along(step), r))
+
     greet_if(r > 0, (d, r - 1))
     greet_if(r < R - 1, (d, r + 1))
-    n_greet = X + 3
+    greet_if((x == 0) & (y > 2) & (y < Y - 2), (0, r))
+    hears_across = (y == 0) & (x > 1)
+    hears_along = (x == 0) & (y > 0)
+    beside_root = (x == 0) & ((y == 1) | (y == 2) | (y == Y - 1) | (y == Y - 2))
+    n_greet = jnp.where(root, X + Y - 2, X + 3 - (hears_across | beside_root).astype(jnp.int32))
     for condition in (crosses_up, crosses_down, r > 0, r < R - 1):
         n_greet = n_greet + condition.astype(jnp.int32)
 
+    tables = [
+        pltpu.make_async_copy(color_map, color_ref, table_sem.at[0]),
+        pltpu.make_async_copy(alpha_map, alpha_ref, table_sem.at[1]),
+    ]
     loads = []
     for p, buffer in enumerate((first, second)):
         for block in range(SUBS):
@@ -70,6 +84,8 @@
             load = pltpu.make_async_copy(source, target, load_sem.at[p, block])
             load.start()
             loads.append(load)
+    for table in tables:
+        table.start()
 
     lane = lax.broadcasted_iota(jnp.int32, (SUBS, LANES), 1)
     sub = lax.broadcasted_iota(jnp.int32, (SUBS, LANES), 0)
@@ -78,10 +94,6 @@
 
     def spread(row):
         return jnp.broadcast_to(row, (SUBS, LANES))
-
-    colors = color_ref[0:1] + color_ref[1:2] * 256 + color_ref[2:3] * 65536
-    color_low, color_high = spread(colors[:, :LANES]), spread(colors[:, LANES:])
-    alphas = spread(alpha_ref[0:1] + alpha_ref[1:2] * 256)
 
     zero = jnp.zeros((SUBS, LANES), jnp.int32)
 
@@ -131,27 +143,34 @@
         def _(copy=copy):
             copy.start()
 
-    for slot, side in ((1, 1), (0, -1)):
-        for hops in (1, 2):
-            pl.semaphore_signal(
-                near_sem.at[slot, hops - 1], inc=1,
-                device_id=(along(side * hops), r), device_id_type=MESH,
-            )
-    side = jnp.where(y <= Y // 2, 1, -1)
-    middle = (y == 0) | ((y >= Y // 2 - 1) & (y <= Y // 2 + 1))
-
-    def slot_of(side):
-        return lax.div(1 - side, 2)
-
-    def hear_near(side):
-        pl.semaphore_wait(near_sem.at[slot_of(side), 0], 1)
-        pl.semaphore_wait(near_sem.at[slot_of(side), 1], 1)
-        pl.semaphore_signal(
-            far_sem.at[slot_of(side)], inc=1, device_id=(along(-2 * side), r), device_id_type=MESH
-        )
-
-    for load in loads[SUBS:]:
+    def tell(semaphore, device):
+        pl.semaphore_signal(semaphore, inc=1, device_id=device, device_id_type=MESH)
+
+    @pl.when(root)
+    def _():
+        for k in range(2, X):
+            tell(here_sem, (k, r))
+        for k in range(1, Y):
+            tell(here_sem, (k * X, r))
+
+    for step in (2, -2):
+        @pl.when(jnp.logical_not(root) & (along(step) != 0))
+        def _(step=step):
+            tell(news_sem, (along(step), r))
+
+    @pl.when((x == 0) & (y == 1))
+    def _():
+        tell(news_sem, (along(1), r))
+
+    @pl.when((x == 0) & (y == Y - 1))
+    def _():
+        tell(news_sem, (along(-1), r))
+
+    for load in tables + loads[SUBS:]:
         load.wait()
+    colors = color_ref[0:1] + color_ref[1:2] * 256 + color_ref[2:3] * 65536
+    color_low, color_high = spread(colors[:, :LANES]), spread(colors[:, LANES:])
+    alphas = spread(alpha_ref[0:1] + alpha_ref[1:2] * 256)
 
     def inner(row):
         clear = jnp.ones((SUBS, LANES), F32)
@@ -193,15 +212,7 @@
             inner(UNROLL * i + 1 + k)
         return 0
 
-    groups = (H - 2) // UNROLL
-    lax.fori_loop(0, groups // 2, inner_group, 0)
-    hear_near(side)
-
-    @pl.when(middle)
-    def _():
-        hear_near(-side)
-
-    lax.fori_loop(groups // 2, groups, inner_group, 0)
+    lax.fori_loop(0, (H - 2) // UNROLL, inner_group, 0)
 
     for copy, _, receives in halos[2:]:
         @pl.when(receives)
@@ -219,7 +230,7 @@
         def _(copy=copy):
             copy.wait_recv()
 
-    def outer(row, buffer, slot):
+    def outer(row, target):
         total = [part[row, i] for i in range(3)]
         word, shift = lax.rem(row, HALF), lax.div(row, HALF) * 16
         front, back = ((depth_halo[i, word] >> shift) & 255 for i in range(2))
@@ -235,70 +246,106 @@
         total.append(part[row, 3])
         for i in range(2):
             pair = jnp.concatenate(total[2 * i : 2 * i + 2], axis=0)
-            buffer[slot, pl.ds(16 * i, 16)] = pair.astype(jnp.bfloat16)
-
-    def shipment(row):
-        return pltpu.make_async_remote_copy(
-            src_ref=sent.at[row], dst_ref=got.at[d], send_sem=send_sem.at[row],
-            recv_sem=recv_sem.at[d], device_id=(row, r), device_id_type=MESH,
-        )
-
-    outer(d, got, d)
-    for k in range(1, X):
-        row = y * X + lax.rem(x + k, X)
-        outer(row, sent, row)
-        shipment(row).start()
+            target[pl.ds(16 * i, 16)] = pair.astype(jnp.bfloat16)
+
+    def block(k):
+        half = lax.div(k + 1, 2)
+        return lax.rem(y + Y // 2 + jnp.where(lax.rem(k, 2) == 1, -half, half), Y)
+
+    def across(at, shift):
+        to = lax.rem(x + shift, X)
+        return pltpu.make_async_remote_copy(
+            src_ref=sent.at[at, to], dst_ref=got.at[at, x], send_sem=sent_sem.at[at, to],
+            recv_sem=got_sem.at[at, x], device_id=(y * X + to, r), device_id_type=MESH,
+        )
+
+    def onward(at):
+        return pltpu.make_async_remote_copy(
+            src_ref=joined.at[at], dst_ref=met.at[y], send_sem=joined_sem.at[at],
+            recv_sem=met_sem.at[y], device_id=(at * X + x, r), device_id_type=MESH,
+        )
+
+    def arrival(at, source):
+        return pltpu.make_async_remote_copy(
+            src_ref=sent.at[at, source], dst_ref=got.at[at, source],
+            send_sem=sent_sem.at[at, source], recv_sem=got_sem.at[at, source],
+            device_id=(y * X + source, r), device_id_type=MESH,
+        )
+
+    def meeting(at):
+        return pltpu.make_async_remote_copy(
+            src_ref=joined.at[at], dst_ref=met.at[at], send_sem=joined_sem.at[at],
+            recv_sem=met_sem.at[at], device_id=(at * X + x, r), device_id_type=MESH,
+        )
+
+    shifts = (2, 1, 3)
 
     def ship(k, _):
-        late = jnp.where(k < 4, k + 2, jnp.where(k < 6, k - 4, k))
-        step = jnp.where(y == Y // 2, late, k)
-
-        @pl.when(step == 0)
+        at = block(k)
+        for shift in shifts:
+            to = lax.rem(x + shift, X)
+            outer(at * X + to, sent.at[at, to])
+        for shift in shifts:
+            across(at, shift).start()
+        outer(at * X + x, got.at[at, x])
+        return 0
+
+    @pl.when(hears_across)
+    def _():
+        pl.semaphore_wait(here_sem, 1)
+
+    lax.fori_loop(0, Y, ship, 0)
+
+    def fold(slabs):
+        clear = jnp.ones((SUBS, LANES), F32)
+        total = [jnp.zeros((SUBS, LANES), F32)] * 3
+        for slab in slabs:
+            total = [t + clear * slab[SUBS * i : SUBS * (i + 1)] for i, t in enumerate(total)]
+            clear = clear - clear * slab[3 * SUBS :]
+        return total + [1.0 - clear]
+
+    def join(at, target):
+        for shift in shifts:
+            arrival(at, lax.rem(x + shift, X)).wait_recv()
+        for i, channel in enumerate(fold([got[at, k].astype(F32) for k in range(X)])):
+            target[pl.ds(SUBS * i, SUBS)] = channel
+
+    @pl.when(hears_along)
+    def _():
+        pl.semaphore_wait(here_sem, 1)
+
+    @pl.when(jnp.logical_not(root))
+    def _():
+        pl.semaphore_wait(news_sem, 2)
+
+    def pass_on(k, _):
+        at = block(k)
+        join(at, joined.at[at])
+        onward(at).start()
+        return 0
+
+    lax.fori_loop(0, Y - 1, pass_on, 0)
+    join(y, met.at[y])
+
+    def meet(k, _):
+        meeting(block(k)).wait_recv()
+        return 0
+
+    lax.fori_loop(0, Y - 1, meet, 0)
+    for i, channel in enumerate(fold([met[k] for k in range(Y)])):
+        out_ref[i] = channel
+
+    def drain(k, _):
+        for shift in shifts:
+            across(k, shift).wait_send()
+
+        @pl.when(k != y)
         def _():
-            pl.semaphore_wait(far_sem.at[slot_of(side)], 1)
-
-        @pl.when((step == 4) & jnp.logical_not(middle))
-        def _():
-            hear_near(-side)
-
-        @pl.when(step == 6)
-        def _():
-            pl.semaphore_wait(far_sem.at[slot_of(-side)], 1)
-
-        away = jnp.where(step < 2, step + 3, jnp.where(step < 4, step - 1, 3 - step))
-        base = lax.rem(y + away * side + Y, Y) * X
-        for i in range(X):
-            outer(base + i, sent, base + i)
-        for i in range(X):
-            shipment(base + i).start()
-        return 0
-
-    lax.fori_loop(0, Y - 1, ship, 0)
-
-    def arrive(k, _):
-        peer = lax.rem(d + k, D)
-        pltpu.make_async_remote_copy(
-            src_ref=sent.at[peer], dst_ref=got.at[peer], send_sem=send_sem.at[peer],
-            recv_sem=recv_sem.at[peer], device_id=(peer, r), device_id_type=MESH,
-        ).wait_recv()
-        return 0
-
-    lax.fori_loop(1, D, arrive, 0)
-
-    clear = jnp.ones((SUBS, LANES), F32)
-    total = [jnp.zeros((SUBS, LANES), F32)] * 3
-    for k in range(D):
-        slab = got[k].astype(F32)
-        total = [t + clear * slab[SUBS * i : SUBS * (i + 1)] for i, t in enumerate(total)]
-        clear = clear - clear * slab[3 * SUBS :]
-    for i, x in enumerate(total + [1.0 - clear]):
-        out_ref[i] = x
-
-    def drain(k, _):
-        shipment(lax.rem(d + k, D)).wait_send()
-        return 0
-
-    lax.fori_loop(1, D, drain, 0)
+            onward(k).wait_send()
+
+        return 0
+
+    lax.fori_loop(0, Y, drain, 0)
     for copy, sends, _ in halos:
         @pl.when(sends)
         def _(copy=copy):
@@ -312,24 +359,31 @@
     image = pl.pallas_call(
         functools.partial(kernel, S, H, D, R),
         out_shape=pltpu.VMEM((4, SUBS, LANES), F32),
-        in_specs=[pl.BlockSpec(memory_space=pl.ANY), vmem, vmem],
+        in_specs=[pl.BlockSpec(memory_space=pl.ANY)] * 3,
         out_specs=vmem,
         scratch_shapes=[
+            pltpu.VMEM(color_map.shape, jnp.int32),
+            pltpu.VMEM((2, LANES), jnp.int32),
             pltpu.VMEM((S, H + 2, SUBS, LANES), jnp.int32),
             pltpu.VMEM((S, H, SUBS, LANES), jnp.int32),
             pltpu.VMEM((2, S, SUBS, LANES), jnp.int32),
             pltpu.VMEM((2, H // 2, SUBS, LANES), jnp.int32),
             pltpu.VMEM((2, H // 2, SUBS, LANES), jnp.int32),
             pltpu.VMEM((H, 16, SUBS, LANES), F32),
-            pltpu.VMEM((D, 4 * SUBS, LANES), jnp.bfloat16),
-            pltpu.VMEM((D, 4 * SUBS, LANES), jnp.bfloat16),
+            pltpu.VMEM((D // X, X, 4 * SUBS, LANES), jnp.bfloat16),
+            pltpu.VMEM((D // X, X, 4 * SUBS, LANES), jnp.bfloat16),
+            pltpu.VMEM((D // X, 4 * SUBS, LANES), F32),
+            pltpu.VMEM((D // X, 4 * SUBS, LANES), F32),
+            pltpu.SemaphoreType.DMA((2,)),
             pltpu.SemaphoreType.DMA((2, SUBS)),
             pltpu.SemaphoreType.DMA((4,)),
             pltpu.SemaphoreType.DMA((4,)),
-            pltpu.SemaphoreType.DMA((D,)),
-            pltpu.SemaphoreType.DMA((D,)),
-            pltpu.SemaphoreType.REGULAR((2, 2)),
-            pltpu.SemaphoreType.REGULAR((2,)),
+            pltpu.SemaphoreType.DMA((D // X, X)),
+            pltpu.SemaphoreType.DMA((D // X, X)),
+            pltpu.SemaphoreType.DMA((D // X,)),
+            pltpu.SemaphoreType.DMA((D // X,)),
+            pltpu.SemaphoreType.REGULAR,
+            pltpu.SemaphoreType.REGULAR,
         ],
         compiler_params=pltpu.CompilerParams(collective_id=0, has_side_effects=True),
         name="render",

time: 26.2 us -> 22.7 us (0.87)
  the two profiles are of different devices: /device:TPU:6 before, /device:TPU:8 now
where the time goes in v3:
time: 22.7 us; the launch traced here: 22.6 us
  Pallas kernels  22 us (97%)
  local copies, waits for them, and re-layouts  0.61 us (3%)
    pallas_call x1, Pallas kernels, body(): pl.pallas_call(functools.partial(kernel, S, H, D, R), out_shape=pltpu.VME...  22 us
    unnamed x1, local copies, waits for them, and re-layouts  0.61 us

profile of v3, /device:TPU:8, one launch (start us, length us, event | category | flops | bytes accessed | tf_op | source)
XLA Modules:
  0.0 22.6 jit_solution(11260557804144727778)
XLA Ops:
  0.0 22.0 %render.1 = f32[4,8,128]{2,1,0:T(8,128)S(1)} custom-call(s32[2,8,32,1024]{3,2,1,0:T(8,128)} %volume.1, s32[3,256]{1,0:T(4,128)} %color_map.1, s32[2,128]{1,0:T(2,128)} %bitcast.3), custom_call_target="tpu_custom_call" | custom-call | tf_op jit(solution)/shard_map/render/pallas_call | solution.py:359
  22.0 0.6 %copy.6 = f32[4,1,1024]{2,1,0:T(1,128)} copy(f32[4,1,1024]{2,1,0:T(1,128)S(1)} %bitcast.2) | data formatting | bytes 32768

commit v4 on v3

v4 whole, which is shorter than its diff:
```python
import functools

import jax
import jax.numpy as jnp
from jax import lax
from jax.experimental import pallas as pl
from jax.experimental.pallas import tpu as pltpu
from jax.sharding import PartitionSpec as P

LIGHT_DEPTH = 0.336
LIGHT_ROWS = 0.42
LIGHT_COLS = 0.448
OPACITY = 4.0
LANES = 128
SUBS = 8
MESH = pl.DeviceIdType.MESH
F32 = jnp.float32
X = 4
UNROLL = 10


def take(table, index):
    return jnp.take_along_axis(table, index, axis=1, mode="promise_in_bounds")


def kernel(
    slices, height, depth_count, row_count,
    volume, color_map, alpha_map, out_ref,
    color_ref, alpha_ref, first, second, row_halo, depth_edge, depth_halo, part, veil_sent, veil_got, sent, got,
    joined, met,
    table_sem, load_sem, halo_send, halo_recv, edge_send, edge_recv, veil_sent_sem, veil_got_sem, sent_sem, got_sem, joined_sem, met_sem, news_sem, here_sem,
):
    S, H, D, R = slices, height, depth_count, row_count
    d, r = lax.axis_index("depth"), lax.axis_index("rows")

    Y = D // X
    y, x = lax.div(d, X), lax.rem(d, X)
    HALF = H // 2

    def along(step):
        return lax.rem(y + step + Y, Y) * X + x

    barrier = pltpu.get_barrier_semaphore()

    def greet(device):
        pl.semaphore_signal(barrier, inc=1, device_id=device, device_id_type=MESH)

    def greet_if(condition, device):
        @pl.when(condition)
        def _():
            greet(device)

    root = d == 0
    crosses_up, crosses_down = (x == X - 1) & (d < D - 1), (x == 0) & (d > 0)
    greet_if(crosses_up, (d + 1, r))
    greet_if(crosses_down, (d - 1, r))
    greet_if(root, (d + 1, r))

    @pl.when(jnp.logical_not(root))
    def _():
        for k in range(1, X):
            greet((y * X + lax.rem(x + k, X), r))
        for step in (1, -1, 2, -2):
            greet((along(step), r))

    greet_if(r > 0, (d, r - 1))
    greet_if(r < R - 1, (d, r + 1))
    greet_if((x == 0) & (y > 2) & (y < Y - 2), (0, r))
    hears_across = (y == 0) & (x > 1)
    hears_along = (x == 0) & (y > 0)
    beside_root = (x == 0) & ((y == 1) | (y == 2) | (y == Y - 1) | (y == Y - 2))
    n_greet = jnp.where(root, X + Y - 2, X + 3 - (hears_across | beside_root).astype(jnp.int32))
    for condition in (crosses_up, crosses_down, r > 0, r < R - 1):
        n_greet = n_greet + condition.astype(jnp.int32)

    tables = [
        pltpu.make_async_copy(color_map, color_ref, table_sem.at[0]),
        pltpu.make_async_copy(alpha_map, alpha_ref, table_sem.at[1]),
    ]
    loads = []
    for p, buffer in enumerate((first, second)):
        for block in range(SUBS):
            source = volume.at[p, :, :, pl.ds(block * LANES, LANES)]
            target = buffer.at[:, pl.ds(1, H), block, :] if p == 0 else buffer.at[:, :, block, :]
            load = pltpu.make_async_copy(source, target, load_sem.at[p, block])
            load.start()
            loads.append(load)
    for table in tables:
        table.start()

    lane = lax.broadcasted_iota(jnp.int32, (SUBS, LANES), 1)
    sub = lax.broadcasted_iota(jnp.int32, (SUBS, LANES), 0)
    last_lane, first_lane = lane == LANES - 1, lane == 0
    not_last, not_first = (sub < SUBS - 1).astype(F32), (sub > 0).astype(F32)

    def spread(row):
        return jnp.broadcast_to(row, (SUBS, LANES))

    zero = jnp.zeros((SUBS, LANES), jnp.int32)

    @pl.when(d == 0)
    def _():
        for i in range(HALF):
            depth_halo[0, i // X, i % X] = zero

    @pl.when(d == D - 1)
    def _():
        for i in range(HALF):
            depth_halo[1, i // X, i % X] = zero

    @pl.when(r == 0)
    def _():
        for s in range(S):
            row_halo[0, s] = zero

    @pl.when(r == R - 1)
    def _():
        for s in range(S):
            row_halo[1, s] = zero

    for load in loads[:SUBS]:
        load.wait()
    def lookups():
        colors = color_ref[0:1] + color_ref[1:2] * 256 + color_ref[2:3] * 65536
        alphas = alpha_ref[...].astype(F32) * (OPACITY / (255.0 * S * D))
        return (
            spread(colors[:, :LANES]), spread(colors[:, LANES:]),
            spread(alphas[0:1]), spread(alphas[1:2]),
        )

    def inner(row, tables):
        color_low, color_high, alpha_low, alpha_high = tables
        clear = jnp.ones((SUBS, LANES), F32)
        total = [jnp.zeros((SUBS, LANES), F32)] * 3
        value = [first[s, row + 1] for s in range(S)]
        for s in range(S):
            level = second[s, row]
            index = level & 127
            opacity = jnp.where(level >= 128, take(alpha_high, index), take(alpha_low, index))
            index = value[s] & 127
            code = jnp.where(value[s] >= 128, take(color_high, index), take(color_low, index))
            emitted = [(code & 255).astype(F32), ((code >> 8) & 255).astype(F32), (code >> 16).astype(F32)]
            here = value[s].astype(F32)
            right = pltpu.roll(here, LANES - 1, 1)
            left = pltpu.roll(here, 1, 1)
            right = jnp.where(last_lane, pltpu.roll(right, SUBS - 1, 0) * not_last, right)
            left = jnp.where(first_lane, pltpu.roll(left, 1, 0) * not_first, left)
            grad_cols = right - left
            grad_rows = (first[s, row + 2] - first[s, row]).astype(F32)
            facing = LIGHT_ROWS * grad_rows + LIGHT_COLS * grad_cols
            square = grad_rows * grad_rows + grad_cols * grad_cols
            weight = clear * opacity
            clear = clear - weight
            if 0 < s < S - 1:
                grad_depth = (value[s + 1] - value[s - 1]).astype(F32)
                facing = facing + LIGHT_DEPTH * grad_depth
                square = square + grad_depth * grad_depth
                lit = weight * (0.3 + jnp.abs(facing) * lax.rsqrt(jnp.maximum(square, 4.0)))
                total = [t + e * lit for t, e in zip(total, emitted)]
            else:
                for i, x in enumerate([weight, facing, square] + emitted):
                    part[row, (4 if s == 0 else 10) + i] = x
        for i, x in enumerate(total + [1.0 - clear]):
            part[row, i] = x

    def interior():
        for load in tables + loads[SUBS:]:
            load.wait()
        looked_up = lookups()

        def inner_group(i, _):
            for k in range(UNROLL):
                inner(UNROLL * i + 1 + k, looked_up)
            return 0

        lax.fori_loop(0, (H - 2) // UNROLL, inner_group, 0)

    computes_first = (d == 1) | (root & (r > 0))

    @pl.when(computes_first)
    def _():
        interior()

    for i in range(HALF):
        depth_edge[0, i // X, i % X] = first[S - 1, i + 1] + first[S - 1, i + 1 + HALF] * 65536
        depth_edge[1, i // X, i % X] = first[0, i + 1] + first[0, i + 1 + HALF] * 65536
    pl.semaphore_wait(barrier, n_greet)

    def halo(which, source, target, device):
        return pltpu.make_async_remote_copy(
            src_ref=source, dst_ref=target, send_sem=halo_send.at[which],
            recv_sem=halo_recv.at[which], device_id=device, device_id_type=MESH,
        )

    def block(k):
        half = lax.div(k + 1, 2)
        return lax.rem(y + Y // 2 + jnp.where(lax.rem(k, 2) == 1, -half, half), Y)

    def edge(which, chunk, device):
        return pltpu.make_async_remote_copy(
            src_ref=depth_edge.at[which, chunk], dst_ref=depth_halo.at[which, chunk],
            send_sem=edge_send.at[which, chunk], recv_sem=edge_recv.at[which, chunk],
            device_id=device, device_id_type=MESH,
        )

    CHUNKS = Y // 2
    edges = (
        (0, (d + 1, r), d < D - 1, d > 0), (1, (d - 1, r), d > 0, d < D - 1),
    )
    for k in range(CHUNKS):
        for which, device, sends, _ in edges:
            @pl.when(sends)
            def _(k=k, which=which, device=device):
                edge(which, lax.rem(block(k), CHUNKS), device).start()
    below = halo(0, first.at[:, H], row_halo.at[0], (d, r + 1))
    above = halo(1, first.at[:, 1], row_halo.at[1], (d, r - 1))
    halos = ((below, r < R - 1, r > 0), (above, r > 0, r < R - 1))
    for copy, sends, _ in halos:
        @pl.when(sends)
        def _(copy=copy):
            copy.start()

    def tell(semaphore, device):
        pl.semaphore_signal(semaphore, inc=1, device_id=device, device_id_type=MESH)

    @pl.when(root)
    def _():
        for k in range(2, X):
            tell(here_sem, (k, r))
        for k in range(1, Y):
            tell(here_sem, (k * X, r))

    for step in (2, -2):
        @pl.when(jnp.logical_not(root) & (along(step) != 0))
        def _(step=step):
            tell(news_sem, (along(step), r))

    @pl.when((x == 0) & (y == 1))
    def _():
        tell(news_sem, (along(1), r))

    @pl.when((x == 0) & (y == Y - 1))
    def _():
        tell(news_sem, (along(-1), r))

    @pl.when(jnp.logical_not(computes_first))
    def _():
        interior()

    for copy, _, receives in halos:
        @pl.when(receives)
        def _(copy=copy):
            copy.wait_recv()
    for s in range(S):
        first[s, 0] = row_halo[0, s]
        first[s, H + 1] = row_halo[1, s]

    looked_up = lookups()
    for row in (0, H - 1):
        inner(row, looked_up)

    def outer(row):
        total = [part[row, i] for i in range(3)]
        chunk, word = lax.rem(lax.div(row, X), CHUNKS), lax.rem(row, X)
        shift = lax.div(row, HALF) * 16
        front, back = ((depth_halo[i, chunk, word] >> shift) & 255 for i in range(2))
        for at, grad in (
            (4, first[1, row + 1] - front),
            (10, back - first[S - 2, row + 1]),
        ):
            grad = grad.astype(F32)
            facing = part[row, at + 1] + LIGHT_DEPTH * grad
            square = part[row, at + 2] + grad * grad
            lit = part[row, at] * (0.3 + jnp.abs(facing) * lax.rsqrt(jnp.maximum(square, 4.0)))
            total = [t + part[row, at + 3 + i] * lit for i, t in enumerate(total)]
        return [t * (1.0 / 255.0) for t in total]

    def two(first_tile, second_tile):
        return jnp.concatenate([first_tile, second_tile], axis=0).astype(jnp.bfloat16)

    shifts = (2, 1, 3)
    PAIRS = Y // 2

    def swap(source, target, send, recv, peer):
        return pltpu.make_async_remote_copy(
            src_ref=source, dst_ref=target, send_sem=send, recv_sem=recv,
            device_id=(y * X + peer, r), device_id_type=MESH,
        )

    def veil(peer, slot):
        return swap(
            veil_sent.at[peer], veil_got.at[slot], veil_sent_sem.at[peer],
            veil_got_sem.at[slot], peer,
        )

    def across(pair, peer, slot):
        return swap(
            sent.at[pair, peer], got.at[pair, slot], sent_sem.at[pair, peer],
            got_sem.at[pair, slot], peer,
        )

    def along_y(at, slot):
        return pltpu.make_async_remote_copy(
            src_ref=joined.at[at], dst_ref=met.at[slot], send_sem=joined_sem.at[at],
            recv_sem=met_sem.at[slot], device_id=(at * X + x, r), device_id_type=MESH,
        )

    @pl.when(hears_across)
    def _():
        pl.semaphore_wait(here_sem, 1)

    for shift in (*shifts, 0):
        peer = lax.rem(x + shift, X)
        target = veil_sent.at[peer] if shift else veil_got.at[x]
        for j in range(PAIRS):
            near, far = block(2 * j) * X + peer, block(2 * j + 1) * X + peer
            target[j] = two(part[near, 3], part[far, 3])
        if shift:
            veil(peer, x).start()

    def ship(j, _):
        pair = (block(2 * j), block(2 * j + 1))
        for at in pair:
            for which, device, _, receives in edges:
                @pl.when(receives & (j < CHUNKS // 2))
                def _(at=at, which=which, device=device):
                    edge(which, lax.rem(at, CHUNKS), device).wait_recv()

        for shift in (*shifts, 0):
            peer = lax.rem(x + shift, X)
            target = sent.at[j, peer] if shift else got.at[j, x]
            channels = zip(*(outer(at * X + peer) for at in pair))
            for i, channel in enumerate(channels):
                target[pl.ds(2 * SUBS * i, 2 * SUBS)] = two(*channel)
        for shift in shifts:
            across(j, lax.rem(x + shift, X), x).start()
        return 0

    lax.fori_loop(0, PAIRS, ship, 0)

    def fold(slabs):
        clear = jnp.ones((SUBS, LANES), F32)
        total = [jnp.zeros((SUBS, LANES), F32)] * 3
        for *colors, opacity in slabs:
            total = [t + clear * c for t, c in zip(total, colors)]
            clear = clear - clear * opacity
        return total + [1.0 - clear]

    @pl.when(hears_along)
    def _():
        pl.semaphore_wait(here_sem, 1)

    @pl.when(jnp.logical_not(root))
    def _():
        pl.semaphore_wait(news_sem, 2)

    for shift in shifts:
        peer = lax.rem(x + shift, X)
        veil(peer, peer).wait_recv()

    for j in range(PAIRS):
        for shift in shifts:
            peer = lax.rem(x + shift, X)
            across(j, peer, peer).wait_recv()
        colors = [got[j, k].astype(F32) for k in range(X)]
        opacities = [veil_got[k, j].astype(F32) for k in range(X)]
        for half in range(2):
            at = block(2 * j + half)
            last = 2 * j + half == Y - 1
            target = met.at[y] if last else joined.at[at]
            low = SUBS * half
            slabs = [
                [c[low + 2 * SUBS * i : low + 2 * SUBS * i + SUBS] for i in range(3)]
                + [o[low : low + SUBS]]
                for c, o in zip(colors, opacities)
            ]
            for i, channel in enumerate(fold(slabs)):
                target[pl.ds(SUBS * i, SUBS)] = channel
            if not last:
                along_y(at, y).start()

    def meet(k, _):
        at = block(k)
        along_y(at, at).wait_recv()
        return 0

    lax.fori_loop(0, Y - 1, meet, 0)
    rows = [met[k] for k in range(Y)]
    rows = [[m[SUBS * i : SUBS * (i + 1)] for i in range(4)] for m in rows]
    for i, channel in enumerate(fold(rows)):
        out_ref[i] = channel

    for shift in shifts:
        peer = lax.rem(x + shift, X)
        veil(peer, x).wait_send()
        for j in range(PAIRS):
            across(j, peer, x).wait_send()

    def drain(k, _):
        along_y(block(k), y).wait_send()
        return 0

    lax.fori_loop(0, Y - 1, drain, 0)
    for copy, sends, _ in halos:
        @pl.when(sends)
        def _(copy=copy):
            copy.wait_send()
    for which, device, sends, _ in edges:
        @pl.when(sends)
        def _(which=which, device=device):
            for chunk in range(CHUNKS):
                edge(which, chunk, device).wait_send()


def body(volume, color_map, alpha_map):
    D, R = lax.axis_size("depth"), lax.axis_size("rows")
    S, H = volume.shape[1], volume.shape[2]
    vmem = pl.BlockSpec(memory_space=pltpu.VMEM)
    image = pl.pallas_call(
        functools.partial(kernel, S, H, D, R),
        out_shape=pltpu.VMEM((4, SUBS, LANES), F32),
        in_specs=[pl.BlockSpec(memory_space=pl.ANY)] * 3,
        out_specs=vmem,
        scratch_shapes=[
            pltpu.VMEM(color_map.shape, jnp.int32),
            pltpu.VMEM((2, LANES), jnp.int32),
            pltpu.VMEM((S, H + 2, SUBS, LANES), jnp.int32),
            pltpu.VMEM((S, H, SUBS, LANES), jnp.int32),
            pltpu.VMEM((2, S, SUBS, LANES), jnp.int32),
            pltpu.VMEM((2, D // X // 2, X, SUBS, LANES), jnp.int32),
            pltpu.VMEM((2, D // X // 2, X, SUBS, LANES), jnp.int32),
            pltpu.VMEM((H, 16, SUBS, LANES), F32),
            pltpu.VMEM((X, D // X // 2, 2 * SUBS, LANES), jnp.bfloat16),
            pltpu.VMEM((X, D // X // 2, 2 * SUBS, LANES), jnp.bfloat16),
            pltpu.VMEM((D // X // 2, X, 6 * SUBS, LANES), jnp.bfloat16),
            pltpu.VMEM((D // X // 2, X, 6 * SUBS, LANES), jnp.bfloat16),
            pltpu.VMEM((D // X, 4 * SUBS, LANES), F32),
            pltpu.VMEM((D // X, 4 * SUBS, LANES), F32),
            pltpu.SemaphoreType.DMA((2,)),
            pltpu.SemaphoreType.DMA((2, SUBS)),
            pltpu.SemaphoreType.DMA((2,)),
            pltpu.SemaphoreType.DMA((2,)),
            pltpu.SemaphoreType.DMA((2, D // X // 2)),
            pltpu.SemaphoreType.DMA((2, D // X // 2)),
            pltpu.SemaphoreType.DMA((X,)),
            pltpu.SemaphoreType.DMA((X,)),
            pltpu.SemaphoreType.DMA((D // X // 2, X)),
            pltpu.SemaphoreType.DMA((D // X // 2, X)),
            pltpu.SemaphoreType.DMA((D // X,)),
            pltpu.SemaphoreType.DMA((D // X,)),
            pltpu.SemaphoreType.REGULAR,
            pltpu.SemaphoreType.REGULAR,
        ],
        compiler_params=pltpu.CompilerParams(collective_id=0, has_side_effects=True),
        name="render",
    )(volume, color_map, alpha_map.reshape(2, LANES))
    return image.reshape(4, 1, SUBS * LANES)


def solution(mesh):
    in_specs = (P(None, "depth", "rows", None), P(), P())
    out_specs = P(None, ("rows", "depth"), None)
    return jax.shard_map(body, mesh=mesh, in_specs=in_specs, out_specs=out_specs, check_vma=False)
```

time: 22.7 us -> 22.4 us (0.987)
  the two profiles are of different devices: /device:TPU:8 before, /device:TPU:193 now
where the time goes in v4:
time: 22.4 us; the launch traced here: 22.3 us
  Pallas kernels  21.7 us (97%)
  local copies, waits for them, and re-layouts  0.61 us (3%)
    pallas_call x1, Pallas kernels, body(): pl.pallas_call(functools.partial(kernel, S, H, D, R), out_shape=pltpu.VME...  21.7 us
    unnamed x1, local copies, waits for them, and re-layouts  0.61 us

profile of v4, /device:TPU:193, one launch (start us, length us, event | category | flops | bytes accessed | tf_op | source)
XLA Modules:
  0.0 22.3 jit_solution(13953900365767977480)
XLA Ops:
  0.0 21.7 %render.1 = f32[4,8,128]{2,1,0:T(8,128)S(1)} custom-call(s32[2,8,32,1024]{3,2,1,0:T(8,128)} %volume.1, s32[3,256]{1,0:T(4,128)} %color_map.1, s32[2,128]{1,0:T(2,128)} %bitcast.3), custom_call_target="tpu_custom_call" | custom-call | tf_op jit(solution)/shard_map/render/pallas_call | solution.py:419
  21.7 0.6 %copy.6 = f32[4,1,1024]{2,1,0:T(1,128)} copy(f32[4,1,1024]{2,1,0:T(1,128)S(1)} %bitcast.2) | data formatting | bytes 32768

commit v5 on v4

--- a/solution.py
+++ b/solution.py
@@ -194,7 +194,7 @@
 
     def block(k):
         half = lax.div(k + 1, 2)
-        return lax.rem(y + Y // 2 + jnp.where(lax.rem(k, 2) == 1, -half, half), Y)
+        return lax.rem(jnp.where(lax.rem(k, 2) == 1, half, Y - half), Y)
 
     def edge(which, chunk, device):
         return pltpu.make_async_remote_copy(
@@ -358,6 +358,16 @@
         peer = lax.rem(x + shift, X)
         veil(peer, peer).wait_recv()
 
+    bound = 1.01 * (1.0 - (1.0 - OPACITY / (S * D)) ** (S * X))
+
+    def encode(channels):
+        codes = [(jnp.sqrt(c * (1.0 / bound)) * 65535.0 + 0.5).astype(jnp.int32) for c in channels]
+        return [codes[i] + codes[i + 1] * 65536 for i in (0, 2)]
+
+    def decode(words):
+        codes = [c.astype(F32) for w in words for c in (w & 65535, (w >> 16) & 65535)]
+        return [c * c * (bound / 65535.0**2) for c in codes]
+
     for j in range(PAIRS):
         for shift in shifts:
             peer = lax.rem(x + shift, X)
@@ -366,27 +376,32 @@
         opacities = [veil_got[k, j].astype(F32) for k in range(X)]
         for half in range(2):
             at = block(2 * j + half)
-            last = 2 * j + half == Y - 1
-            target = met.at[y] if last else joined.at[at]
             low = SUBS * half
             slabs = [
                 [c[low + 2 * SUBS * i : low + 2 * SUBS * i + SUBS] for i in range(3)]
                 + [o[low : low + SUBS]]
                 for c, o in zip(colors, opacities)
             ]
-            for i, channel in enumerate(fold(slabs)):
-                target[pl.ds(SUBS * i, SUBS)] = channel
-            if not last:
+            words = encode(fold(slabs))
+
+            @pl.when(at == y)
+            def _(words=words):
+                for i, word in enumerate(words):
+                    met[y, i] = word
+
+            @pl.when(at != y)
+            def _(at=at, words=words):
+                for i, word in enumerate(words):
+                    joined[at, i] = word
                 along_y(at, y).start()
 
     def meet(k, _):
-        at = block(k)
+        at = lax.rem(y + k, Y)
         along_y(at, at).wait_recv()
         return 0
 
-    lax.fori_loop(0, Y - 1, meet, 0)
-    rows = [met[k] for k in range(Y)]
-    rows = [[m[SUBS * i : SUBS * (i + 1)] for i in range(4)] for m in rows]
+    lax.fori_loop(1, Y, meet, 0)
+    rows = [decode([met[k, i] for i in range(2)]) for k in range(Y)]
     for i, channel in enumerate(fold(rows)):
         out_ref[i] = channel
 
@@ -397,10 +412,10 @@
             across(j, peer, x).wait_send()
 
     def drain(k, _):
-        along_y(block(k), y).wait_send()
+        along_y(lax.rem(y + k, Y), y).wait_send()
         return 0
 
-    lax.fori_loop(0, Y - 1, drain, 0)
+    lax.fori_loop(1, Y, drain, 0)
     for copy, sends, _ in halos:
         @pl.when(sends)
         def _(copy=copy):
@@ -434,8 +449,8 @@
             pltpu.VMEM((X, D // X // 2, 2 * SUBS, LANES), jnp.bfloat16),
             pltpu.VMEM((D // X // 2, X, 6 * SUBS, LANES), jnp.bfloat16),
             pltpu.VMEM((D // X // 2, X, 6 * SUBS, LANES), jnp.bfloat16),
-            pltpu.VMEM((D // X, 4 * SUBS, LANES), F32),
-            pltpu.VMEM((D // X, 4 * SUBS, LANES), F32),
+            pltpu.VMEM((D // X, 2, SUBS, LANES), jnp.int32),
+            pltpu.VMEM((D // X, 2, SUBS, LANES), jnp.int32),
             pltpu.SemaphoreType.DMA((2,)),
             pltpu.SemaphoreType.DMA((2, SUBS)),
             pltpu.SemaphoreType.DMA((2,)),

time: 22.4 us -> 22 us (0.982)
  the two profiles are of different devices: /device:TPU:193 before, /device:TPU:34 now
where the time goes in v5:
time: 22 us; the launch traced here: 21.9 us
  Pallas kernels  21.3 us (97%)
  local copies, waits for them, and re-layouts  0.61 us (3%)
    pallas_call x1, Pallas kernels, body(): pl.pallas_call(functools.partial(kernel, S, H, D, R), out_shape=pltpu.VME...  21.3 us
    unnamed x1, local copies, waits for them, and re-layouts  0.61 us

profile of v5, /device:TPU:34, one launch (start us, length us, event | category | flops | bytes accessed | tf_op | source)
XLA Modules:
  0.0 21.9 jit_solution(466317350364682691)
XLA Ops:
  0.0 21.3 %render.1 = f32[4,8,128]{2,1,0:T(8,128)S(1)} custom-call(s32[2,8,32,1024]{3,2,1,0:T(8,128)} %volume.1, s32[3,256]{1,0:T(4,128)} %color_map.1, s32[2,128]{1,0:T(2,128)} %bitcast.3), custom_call_target="tpu_custom_call" | custom-call | tf_op jit(solution)/shard_map/render/pallas_call | solution.py:434
  21.3 0.6 %copy.6 = f32[4,1,1024]{2,1,0:T(1,128)} copy(f32[4,1,1024]{2,1,0:T(1,128)S(1)} %bitcast.2) | data formatting | bytes 32768

commit v6 on v5

--- a/solution.py
+++ b/solution.py
@@ -194,7 +194,11 @@
 
     def block(k):
         half = lax.div(k + 1, 2)
-        return lax.rem(jnp.where(lax.rem(k, 2) == 1, half, Y - half), Y)
+        most = lax.rem(jnp.where(lax.rem(k, 2) == 1, half, Y - half), Y)
+        first_row = lax.rem(k + 1, Y)
+        for at, k_of in ((4, 0), (1, 1), (3, 2), (2, 3)):
+            first_row = jnp.where(k == k_of, at, first_row)
+        return jnp.where(y == 0, first_row, most)
 
     def edge(which, chunk, device):
         return pltpu.make_async_remote_copy(

time: 22 us -> 21.8 us (level)
  the two profiles are of different devices: /device:TPU:34 before, /device:TPU:18 now
where the time goes in v6:
time: 21.8 us; the launch traced here: 21.6 us
  Pallas kernels  21 us (96%)
  local copies, waits for them, and re-layouts  0.61 us (3%)
    pallas_call x1, Pallas kernels, body(): pl.pallas_call(functools.partial(kernel, S, H, D, R), out_shape=pltpu.VME...  21 us
    unnamed x1, local copies, waits for them, and re-layouts  0.61 us

profile of v6, /device:TPU:18, one launch (start us, length us, event | category | flops | bytes accessed | tf_op | source)
XLA Modules:
  0.0 21.6 jit_solution(5171098735580667201)
XLA Ops:
  0.0 21.0 %render.1 = f32[4,8,128]{2,1,0:T(8,128)S(1)} custom-call(s32[2,8,32,1024]{3,2,1,0:T(8,128)} %volume.1, s32[3,256]{1,0:T(4,128)} %color_map.1, s32[2,128]{1,0:T(2,128)} %bitcast.3), custom_call_target="tpu_custom_call" | custom-call | tf_op jit(solution)/shard_map/render/pallas_call | solution.py:438
  21.0 0.6 %copy.6 = f32[4,1,1024]{2,1,0:T(1,128)} copy(f32[4,1,1024]{2,1,0:T(1,128)S(1)} %bitcast.2) | data formatting | bytes 32768

commit v7 on v6

--- a/solution.py
+++ b/solution.py
@@ -16,7 +16,7 @@
 MESH = pl.DeviceIdType.MESH
 F32 = jnp.float32
 X = 4
-UNROLL = 10
+UNROLL = 6
 
 
 def take(table, index):

time: 21.8 us -> 21.9 us (level)
  no operation moved by 1% of the time
where the time goes in v7:
time: 21.9 us; the launch traced here: 21.8 us
  Pallas kernels  21.1 us (96%)
  local copies, waits for them, and re-layouts  0.61 us (3%)
    pallas_call x1, Pallas kernels, body(): pl.pallas_call(functools.partial(kernel, S, H, D, R), out_shape=pltpu.VME...  21.1 us
    unnamed x1, local copies, waits for them, and re-layouts  0.61 us

profile of v7, /device:TPU:18, one launch (start us, length us, event | category | flops | bytes accessed | tf_op | source)
XLA Modules:
  0.0 21.8 jit_solution(65546278679238970)
XLA Ops:
  0.0 21.1 %render.1 = f32[4,8,128]{2,1,0:T(8,128)S(1)} custom-call(s32[2,8,32,1024]{3,2,1,0:T(8,128)} %volume.1, s32[3,256]{1,0:T(4,128)} %color_map.1, s32[2,128]{1,0:T(2,128)} %bitcast.3), custom_call_target="tpu_custom_call" | custom-call | tf_op jit(solution)/shard_map/render/pallas_call | solution.py:438
  21.2 0.6 %copy.6 = f32[4,1,1024]{2,1,0:T(1,128)} copy(f32[4,1,1024]{2,1,0:T(1,128)S(1)} %bitcast.2) | data formatting | bytes 32768
